TPU v7x, 512 devices: a whole 4x8x8 slice. The times are simulated.
512 devices in a mesh: ctx: 64 (over z, y), tp: 8 (over x, core).
Axes of the slice: x: 4, y: 8, z: 8, core: 2. Of those that a mesh axis runs over, the one named last changes fastest.
Arguments:
- span_q: bfloat16 [8192, 8192], P('ctx', 'tp'), may hold values from -21 to 21
- span_kv: bfloat16 [2, 8192, 1024], P(None, 'ctx', 'tp'), may hold values from -20 to 20
- cache_kv: bfloat16 [2, 65536, 1024], P(None, 'ctx', 'tp'), may hold values from -20 to 20
- anchor_kv: bfloat16 [2, 2048, 1024], P(None, 'ctx', 'tp'), may hold values from -20 to 20
- block_len: int32 [64], P('ctx'), may hold values from 1 to 1024, 40960 in all
- queries: bfloat16 [128, 8192], P('ctx', 'tp'), may hold values from -21 to 21
- out_weight: bfloat16 [8192, 8192], P('tp', 'ctx'), may hold values from -0.0625 to 0.0625
Outputs:
- span_out: bfloat16 [8192, 8192], P('ctx', 'tp')
- answer: bfloat16 [128, 8192], P('tp', 'ctx')
Inputs may be any that keep to these rules, and one draw needn't show every extreme that they name: The new tokens of block c follow its block_len[c] valid cache rows.
All inputs are finite; a program needn't handle non-finite values.
Results may differ from a plain program's by a relative error of at most 0.0049.
Values may be sent and summed in bfloat16 or wider, within the bound.
A program may use at most 64 MiB of HBM per device.

v0:
```python
import math
import jax
import jax.numpy as jnp
from jax import lax
from jax.sharding import PartitionSpec as P

HD = 128
masked_score = -1e30


def all_heads(query_rows, key_rows, value_rows, visible):
    row_count = query_rows.shape[0]
    head_count = query_rows.shape[1] // HD
    score_scale = 1.0 / math.sqrt(HD)

    def per_head(head_index, running):
        maxima, totals, outputs = running
        q_head = lax.dynamic_slice_in_dim(query_rows, head_index * HD, HD, 1)
        scores = (
            jnp.einsum("qd,nd->qn", q_head, key_rows, preferred_element_type=jnp.float32)
            * score_scale
        )
        scores = jnp.where(visible, scores, masked_score)
        peak_score = jnp.max(scores, axis=1, keepdims=True)
        weights = jnp.exp(scores - peak_score)
        weight_sum = jnp.sum(weights, axis=1, keepdims=True)
        product = jnp.einsum(
            "qn,nd->qd",
            weights.astype(jnp.bfloat16),
            value_rows,
            preferred_element_type=jnp.float32,
        )
        maxima = lax.dynamic_update_slice_in_dim(maxima, peak_score, head_index, 1)
        totals = lax.dynamic_update_slice_in_dim(totals, weight_sum, head_index, 1)
        outputs = lax.dynamic_update_slice_in_dim(outputs, product, head_index * HD, 1)
        return (maxima, totals, outputs)

    initial = (
        jnp.zeros((row_count, head_count), jnp.float32),
        jnp.zeros((row_count, head_count), jnp.float32),
        jnp.zeros((row_count, head_count * HD), jnp.float32),
    )
    return lax.fori_loop(0, head_count, per_head, initial)


def local(span_q, span_kv, cache_kv, anchor_kv, block_len, queries, out_weight):
    cache_count = cache_kv.shape[1]
    span_count = span_kv.shape[1]
    length = block_len[0]
    local_kv = jnp.concatenate([cache_kv, span_kv], axis=1)
    anchor_all = lax.all_gather(anchor_kv, "ctx", axis=1, tiled=True)
    query_all = lax.all_gather(queries, "ctx", axis=0, tiled=True)
    anchor_count = anchor_all.shape[1]
    first_kv = jnp.concatenate([anchor_all, local_kv], axis=1)
    key_total = first_kv.shape[1]
    column = lax.broadcasted_iota(jnp.int32, (span_count, key_total), 1)
    query_pos = lax.broadcasted_iota(jnp.int32, (span_count, key_total), 0)
    in_cache = (column >= anchor_count) & (column < anchor_count + cache_count)
    in_span = column >= anchor_count + cache_count
    visible = jnp.where(
        in_cache,
        column - anchor_count < length,
        jnp.where(in_span, column - anchor_count - cache_count <= query_pos, True),
    )
    first_max, first_sum, first_values = all_heads(span_q, first_kv[0], first_kv[1], visible)
    span_out = (first_values / jnp.repeat(first_sum, HD, axis=1)).astype(jnp.bfloat16)
    own_count = anchor_kv.shape[1]
    second_kv = jnp.concatenate([anchor_kv, local_kv], axis=1)
    column_two = lax.broadcasted_iota(jnp.int32, (1, second_kv.shape[1]), 1)
    cache_two = (column_two >= own_count) & (column_two < own_count + cache_count)
    visible_two = jnp.where(cache_two, column_two - own_count < length, True)
    part_max, part_sum, part_values = all_heads(query_all, second_kv[0], second_kv[1], visible_two)
    global_max = lax.pmax(part_max, "ctx")
    rescale = jnp.exp(part_max - global_max)
    full_sum, full_values = lax.psum(
        (part_sum * rescale, part_values * jnp.repeat(rescale, HD, axis=1)), "ctx"
    )
    attended = (full_values / jnp.repeat(full_sum, HD, axis=1)).astype(jnp.bfloat16)
    partial_value = jnp.dot(attended, out_weight, preferred_element_type=jnp.float32)
    answer = lax.psum_scatter(partial_value, "tp", scatter_dimension=0, tiled=True).astype(
        jnp.bfloat16
    )
    return (span_out, answer)


def solution(mesh):
    placed = (
        P("ctx", "tp"),
        P(None, "ctx", "tp"),
        P(None, "ctx", "tp"),
        P(None, "ctx", "tp"),
        P("ctx"),
        P("ctx", "tp"),
        P("tp", "ctx"),
    )
    return jax.shard_map(
        local,
        mesh=mesh,
        in_specs=placed,
        out_specs=(P("ctx", "tp"), P("tp", "ctx")),
        check_vma=False,
    )
```

profile of v0, /device:TPU:16, one launch (start us, length us, event | category | flops | bytes accessed | tf_op | source)
XLA Modules:
  0.0 452.8 jit_solution(17501054155772972104)
XLA Ops:
  7.2 0.7 all-gather.3.cloned.1.call-update
  8.0 56.4 %all-gather = bf16[64,2,1024]{2,1,0:T(2,128)(2,1)S(1)} all-gather(bf16[1,2,1024]{2,1,0:T(2,128)(2,1)} %bitcast.53), channel_id=1, replica_groups=mesh['ctx'=64,'tp'=8] {'ctx'}, dimensions={0}, use_global_device_ids=true | all-gather | bytes 266240 | tf_op jit(solution)/shard_map/all_gather | solution.py:52
  65.2 0.7 constant_dynamic-update-slice_fusion.5
  65.9 0.6 iota_add_fusion
  66.5 27.6 %all-gather.3.cloned.1.call-done = bf16[2,2048,128]{2,1,0:T(8,128)(2,1)} async-done(((bf16[2,32,128]{2,1,0:T(8,128)(2,1)}), bf16[2,2048,128]{2,1,0:T(8,128)(2,1)}) %all-gather.3.cloned.1.call-update) | async-done | bytes 1048592 | tf_op jit(solution)/shard_map/all_gather | solution.py:51
  94.1 1.3 constant_dynamic-update-slice_fusion.2
  95.7 0.8 copy-done.1
  96.5 1.1 slice_bitcast_fusion.2
  97.6 13.0 %while.35 = (s32[]{:T(128)}, f32[128,8]{0,1:T(8,128)S(1)}, f32[128,8]{0,1:T(8,128)S(1)}, f32[128,1024]{1,0:T(8,128)S(1)}, bf16[128,1024]{1,0:T(8,128)(2,1)S(1)},...) while((s32[]{:T(128)}, f32[128,8]{0,1:T(8,128)S(1)}, ...), condition=%wide.region_7.8_spmd.clone, body=%wide.region_4.7_spmd.clone.sunk | while | flops 78662336 | bytes 2530647 | solution.py:43
  97.7 0.7 select_reduce_fusion.2
  99.3 0.7 select_reduce_fusion.2
  100.9 0.7 select_reduce_fusion.2
  102.5 0.7 select_reduce_fusion.2
  104.2 0.7 select_reduce_fusion.2
  105.8 0.7 select_reduce_fusion.2
  107.4 0.7 select_reduce_fusion.2
  109.0 0.7 select_reduce_fusion.2
  110.6 137.7 %pmax.7 = f32[128,8]{0,1:T(8,128)S(1)} all-reduce(f32[128,8]{0,1:T(8,128)S(1)} %get-tuple-element.271), channel_id=1, replica_groups=mesh['ctx'=64,'tp'=8] {'ctx'}, use_global_device_ids=true, to_apply=%region_8.9 | all-reduce | flops 1024 | bytes 8192 | tf_op jit(solution)/shard_map/pmax | solution.py:73
  248.6 0.9 bitcast_multiply_fusion
  249.8 19.4 %while.34 = (s32[]{:T(128)}, f32[128,8]{0,1:T(8,128)S(1)}, f32[128,1024]{1,0:T(8,128)S(1)}, bf16[128,1024]{1,0:T(8,128)(2,1)}, bf16[3200,128]{1,0:T(8,128)(2,1)S...) while((s32[]{:T(128)}, f32[128,8]{0,1:T(8,128)S(1)}, ...), condition=%wide.region_3.4_spmd.clone, body=%wide.region_0.3_spmd.clone.sunk | while | flops 213810944 | bytes 6681151 | solution.py:43
  249.9 1.5 fusion.46
  251.4 0.5 convolution_dynamic-update-slice_fusion.4
  251.8 0.4 fusion.47
  252.3 1.5 fusion.46
  253.8 0.5 convolution_dynamic-update-slice_fusion.4
  254.3 0.4 fusion.47
  254.7 1.5 fusion.46
  256.2 0.5 convolution_dynamic-update-slice_fusion.4
  256.7 0.4 fusion.47
  257.1 1.5 fusion.46
  258.6 0.5 convolution_dynamic-update-slice_fusion.4
  259.1 0.4 fusion.47
  259.5 1.5 fusion.46
  261.1 0.5 convolution_dynamic-update-slice_fusion.4
  261.5 0.4 fusion.47
  262.0 1.5 fusion.46
  263.5 0.5 convolution_dynamic-update-slice_fusion.4
  263.9 0.4 fusion.47
  264.4 1.5 fusion.46
  265.9 0.5 convolution_dynamic-update-slice_fusion.4
  266.8 1.5 fusion.46
  268.3 0.5 convolution_dynamic-update-slice_fusion.4
  268.8 0.4 fusion.47
  269.2 138.1 %psum.15 = f32[128,8]{0,1:T(8,128)S(1)} all-reduce(f32[128,8]{0,1:T(8,128)S(1)} %get-tuple-element.354), channel_id=1, replica_groups=mesh['ctx'=64,'tp'=8] {'ctx'}, use_global_device_ids=true, to_apply=%region_10.11 | all-reduce | flops 1024 | bytes 8192 | tf_op jit(solution)/shard_map/psum | solution.py:75
  407.7 1.9 fusion.22
  409.8 0.8 fusion.21
  410.6 34.3 %reduce-scatter.2.cloned.1.call-done = f32[16,128]{1,0:T(8,128)} async-done(((f32[128,128]{1,0:T(8,128)}), f32[16,128]{1,0:T(8,128)}) %reduce-scatter.2.cloned.1.call-update) | async-done | bytes 8208 | tf_op jit(solution)/shard_map/reduce_scatter | solution.py:80
  444.9 1.3 convert_element_type.25
  (80 shorter events, 9.6 us)
Async XLA Ops:
  7.2 400.5 %copy-start = (bf16[1024,128]{1,0:T(8,128)(2,1)S(1)}, bf16[1024,128]{1,0:T(8,128)(2,1)}, u32[]{:S(2)}) copy-start(bf16[1024,128]{1,0:T(8,128)(2,1)} %param.17) | copy-start | bytes 786436
  7.2 88.2 %copy-start.2 = (bf16[2,1024,128]{2,1,0:T(8,128)(2,1)S(1)}, bf16[2,1024,128]{2,1,0:T(8,128)(2,1)}, u32[]{:S(2)}) copy-start(bf16[2,1024,128]{2,1,0:T(8,128)(2,1)} %param.13) | copy-start | bytes 1572868
  7.2 86.9 %all-gather.3.cloned.1.call-start = ((), (), s32[]{:S(2)}) async-start(), calls=%async_computation.1 | async-start | bytes 1064960 | tf_op jit(solution)/shard_map/all_gather | solution.py:51
  7.9 399.6 %all-reduce.2.cloned.1.call-start = ((), (), s32[]{:S(2)}) async-start(), calls=%async_computation.2 | async-start | bytes 1048576 | tf_op jit(solution)/shard_map/psum | solution.py:75
  66.5 29.1 %copy-start.3 = (bf16[2,128,128]{2,1,0:T(8,128)(2,1)S(1)}, bf16[2,128,128]{2,1,0:T(8,128)(2,1)}, u32[]{:S(2)}) copy-start(bf16[2,128,128]{2,1,0:T(8,128)(2,1)} %param.12) | copy-start | bytes 196612
  95.7 0.8 copy-start.1
  249.6 195.3 %reduce-scatter.2.cloned.1.call-start = ((), (), s32[]{:S(2)}) async-start(), calls=%async_computation.3 | async-start | bytes 73728 | tf_op jit(solution)/shard_map/reduce_scatter | solution.py:80
Sparse Core Ops, SparseCore 0:
  11.0 83.0 all-gather.2
  249.7 155.1 all-reduce.1
  409.7 35.1 reduce-scatter.1
where the time goes:
time: 454 us; the launch traced here: 453 us
  blocking collectives  332 us (73%)
  waiting for transfers between devices  62.6 us (14%)
  matrix products  23.1 us (5%)
  between operations  14.6 us (3%)
  other arithmetic  13.6 us (3%)
  local copies, waits for them, and re-layouts  6.12 us (1%)
    psum x1, blocking collectives, local(): lax.psum((part_sum * rescale, part_values * jnp.repeat(rescale, HD, axis=...  138 us
    pmax x1, blocking collectives, local(): global_max = lax.pmax(part_max, 'ctx')  138 us
    all_gather x1, blocking collectives, local(): query_all = lax.all_gather(queries, 'ctx', axis=0, tiled=True)  56.4 us
    reduce_scatter x1, waiting for transfers between devices, local(): lax.psum_scatter(partial_value, 'tp', scatter_dimension=0, tiled=True)  34.3 us
    all_gather x1, waiting for transfers between devices, local(): anchor_all = lax.all_gather(anchor_kv, 'ctx', axis=1, tiled=True)  27.6 us
    dot_general x16, matrix products, per_head(): jnp.einsum('qd,nd->qn', q_head, key_rows, preferred_element_type=jnp.floa...  15.1 us
  transfers between devices with their start and end apart: 3, of which 2 were waited for; matrix products, arithmetic and copies ran while one was open for 5% of the time, Pallas kernels for 0%

commit v1 on v0

--- a/solution.py
+++ b/solution.py
@@ -48,7 +48,9 @@
     span_count = span_kv.shape[1]
     length = block_len[0]
     local_kv = jnp.concatenate([cache_kv, span_kv], axis=1)
-    anchor_all = lax.all_gather(anchor_kv, "ctx", axis=1, tiled=True)
+    anchor_all = jnp.concatenate(
+        lax.all_to_all(jnp.stack([anchor_kv] * lax.axis_size("ctx")), "ctx", 0, 0), axis=1
+    )
     query_all = lax.all_gather(queries, "ctx", axis=0, tiled=True)
     anchor_count = anchor_all.shape[1]
     first_kv = jnp.concatenate([anchor_all, local_kv], axis=1)

time: 454 us -> 477 us (1.051)
  the two profiles are of different devices: /device:TPU:16 before, /device:TPU:8 now
where the time goes in v1:
time: 477 us
  blocking collectives  347 us (73%)
  waiting for transfers between devices  45.4 us (10%)
  matrix products  31.2 us (7%)
  starting transfers between devices  16.8 us (4%)
  other arithmetic  15.4 us (3%)
  between operations  14.9 us (3%)
  local copies, waits for them, and re-layouts  5.87 us (1%)
    psum x1, blocking collectives, local(): lax.psum((part_sum * rescale, part_values * jnp.repeat(rescale, HD, axis=...  141 us
    pmax x1, blocking collectives, local(): global_max = lax.pmax(part_max, 'ctx')  138 us
    all_gather x1, blocking collectives, local(): query_all = lax.all_gather(queries, 'ctx', axis=0, tiled=True)  67.7 us
    reduce_scatter x1, waiting for transfers between devices, local(): lax.psum_scatter(partial_value, 'tp', scatter_dimension=0, tiled=True)  33.5 us
    dot_general x16, matrix products, per_head(): jnp.einsum('qd,nd->qn', q_head, key_rows, preferred_element_type=jnp.floa...  18.3 us
    all_to_all x1, starting transfers between devices, local(): lax.all_to_all(jnp.stack([anchor_kv] * lax.axis_size('ctx')), 'ctx', 0, 0)  16.7 us
    psum x1, waiting for transfers between devices, local(): lax.psum((part_sum * rescale, part_values * jnp.repeat(rescale, HD, axis=...  11.8 us
    dot_general x16, matrix products, per_head(): jnp.einsum('qn,nd->qd', weights.astype(jnp.bfloat16), value_rows, preferr...  11.1 us
  transfers between devices with their start and end apart: 3, of which 2 were waited for; matrix products, arithmetic and copies ran while one was open for 5% of the time, Pallas kernels for 0%

profile of v1, /device:TPU:8, one launch (start us, length us, event | category | flops | bytes accessed | tf_op | source)
XLA Modules:
  0.0 476.6 jit_solution(17999498950630288683)
XLA Ops:
  7.2 2.0 stack.2
  9.2 16.7 %all-to-all-start = ((bf16[64,2,32,128]{3,2,1,0:T(8,128)(2,1)}), bf16[64,2,32,128]{3,2,1,0:T(8,128)(2,1)S(1)}, u32[]{:S(2)}, u32[]{:S(2)}) async-start(bf16[64,2,32,128]{3,2,1,0:T(8,128)(2,1)} %stack.2), calls=%async_computation | async-start | bytes 2097152 | tf_op jit(solution)/shard_map/all_to_all | solution.py:52
  26.0 67.7 %all-gather = bf16[64,2,1024]{2,1,0:T(2,128)(2,1)S(1)} all-gather(bf16[1,2,1024]{2,1,0:T(2,128)(2,1)S(1)} %bitcast.57), channel_id=1, replica_groups=mesh['ctx'=64,'tp'=8] {'ctx'}, dimensions={0}, use_global_device_ids=true | all-gather | bytes 266240 | tf_op jit(solution)/shard_map/all_gather | solution.py:54
  94.0 0.9 broadcast.95.clone.1
  94.9 17.8 %while.35 = (s32[]{:T(128)}, f32[128,8]{0,1:T(8,128)S(1)}, f32[128,8]{0,1:T(8,128)S(1)}, f32[128,1024]{1,0:T(8,128)}, bf16[128,1024]{1,0:T(8,128)(2,1)S(1)}, /*i...) while((s32[]{:T(128)}, f32[128,8]{0,1:T(8,128)S(1)}, ...), condition=%wide.region_7.8_spmd.clone, body=%wide.region_4.7_spmd.clone.sunk | while | flops 78662336 | bytes 2530655 | solution.py:43
  94.9 0.7 select_reduce_fusion.2
  96.2 0.9 convolution_dynamic-update-slice_fusion.5
  97.1 0.7 select_reduce_fusion.2
  98.4 0.9 convolution_dynamic-update-slice_fusion.5
  99.4 0.7 select_reduce_fusion.2
  100.6 0.9 convolution_dynamic-update-slice_fusion.5
  101.6 0.7 select_reduce_fusion.2
  102.9 0.9 convolution_dynamic-update-slice_fusion.5
  103.8 0.7 select_reduce_fusion.2
  105.1 0.9 convolution_dynamic-update-slice_fusion.5
  106.0 0.7 select_reduce_fusion.2
  107.3 0.9 convolution_dynamic-update-slice_fusion.5
  108.2 0.7 select_reduce_fusion.2
  109.5 0.9 convolution_dynamic-update-slice_fusion.5
  110.5 0.7 select_reduce_fusion.2
  111.7 1.0 convolution_dynamic-update-slice_fusion.5
  112.7 137.9 %pmax.7 = f32[128,8]{0,1:T(8,128)S(1)} all-reduce(f32[128,8]{0,1:T(8,128)S(1)} %get-tuple-element.271), channel_id=1, replica_groups=mesh['ctx'=64,'tp'=8] {'ctx'}, use_global_device_ids=true, to_apply=%region_8.9 | all-reduce | flops 1024 | bytes 8192 | tf_op jit(solution)/shard_map/pmax | solution.py:75
  250.9 2.0 bitcast_multiply_fusion
  253.6 141.2 %psum.15 = f32[128,8]{0,1:T(8,128)S(1)} all-reduce(f32[128,8]{0,1:T(8,128)S(1)} %get-tuple-element.354), channel_id=1, replica_groups=mesh['ctx'=64,'tp'=8] {'ctx'}, use_global_device_ids=true, to_apply=%region_10.11 | all-reduce | flops 1024 | bytes 8192 | tf_op jit(solution)/shard_map/psum | solution.py:77
  394.9 0.6 iota_compare_fusion.1
  395.5 11.8 %all-reduce.2.cloned.1.call-done = f32[128,1024]{1,0:T(8,128)} async-done(((f32[128,1024]{1,0:T(8,128)}), f32[128,1024]{1,0:T(8,128)}) %all-reduce.2.cloned.1.call-update) | async-done | bytes 524304 | tf_op jit(solution)/shard_map/psum | solution.py:77
  407.5 1.9 fusion.22
  409.4 0.6 fusion.24
  410.0 33.5 %reduce-scatter.2.cloned.1.call-done = f32[16,128]{1,0:T(8,128)} async-done(((f32[128,128]{1,0:T(8,128)}), f32[16,128]{1,0:T(8,128)}) %reduce-scatter.2.cloned.1.call-update) | async-done | bytes 8208 | tf_op jit(solution)/shard_map/reduce_scatter | solution.py:82
  443.6 1.3 convert_element_type.25
  445.1 1.0 slice_bitcast_fusion
  446.2 22.5 %while.34 = (s32[]{:T(128)}, f32[128,8]{0,1:T(8,128)S(1)}, f32[128,1024]{1,0:T(8,128)S(1)}, bf16[128,1024]{1,0:T(8,128)(2,1)}, bf16[3200,128]{1,0:T(8,128)(2,1)}...) while((s32[]{:T(128)}, f32[128,8]{0,1:T(8,128)S(1)}, ...), condition=%wide.region_3.4_spmd.clone, body=%wide.region_0.3_spmd.clone.sunk | while | flops 213810944 | bytes 6677575 | solution.py:43
  446.2 1.9 fusion.46
  449.0 1.9 fusion.46
  451.3 0.4 convolution_dynamic-update-slice_fusion.4
  451.8 1.9 fusion.46
  454.1 0.4 convolution_dynamic-update-slice_fusion.4
  454.6 1.9 fusion.46
  457.0 0.4 convolution_dynamic-update-slice_fusion.4
  457.4 1.9 fusion.46
  459.8 0.4 convolution_dynamic-update-slice_fusion.4
  460.2 1.9 fusion.46
  462.6 0.4 convolution_dynamic-update-slice_fusion.4
  463.0 1.9 fusion.46
  465.4 0.4 convolution_dynamic-update-slice_fusion.4
  465.9 1.9 fusion.46
  468.2 0.4 convolution_dynamic-update-slice_fusion.4
  469.0 0.8 fusion.21
  (89 shorter events, 10.1 us)
Async XLA Ops:
  7.2 400.3 %copy-start = (bf16[1024,128]{1,0:T(8,128)(2,1)S(1)}, bf16[1024,128]{1,0:T(8,128)(2,1)}, u32[]{:S(2)}) copy-start(bf16[1024,128]{1,0:T(8,128)(2,1)} %param.17) | copy-start | bytes 786436
  7.2 18.8 %copy-start.3 = (bf16[2,32,128]{2,1,0:T(8,128)(2,1)S(1)}, bf16[2,32,128]{2,1,0:T(8,128)(2,1)}, u32[]{:S(2)}) copy-start(bf16[2,32,128]{2,1,0:T(8,128)(2,1)} %param.14) | copy-start | bytes 49156
  7.2 18.8 %copy-start.4 = (bf16[2,1024]{1,0:T(2,128)(2,1)S(1)}, bf16[2,1024]{1,0:T(2,128)(2,1)}, u32[]{:S(2)}) copy-start(bf16[2,1024]{1,0:T(2,128)(2,1)} %param.16) | copy-start | bytes 12292
  9.2 84.6 %copy-start.1 = (bf16[2,1024,128]{2,1,0:T(8,128)(2,1)S(1)}, bf16[2,1024,128]{2,1,0:T(8,128)(2,1)}, u32[]{:S(2)}) copy-start(bf16[2,1024,128]{2,1,0:T(8,128)(2,1)} %param.13) | copy-start | bytes 1572868
  9.2 84.7 %copy-start.2 = (bf16[2,128,128]{2,1,0:T(8,128)(2,1)S(1)}, bf16[2,128,128]{2,1,0:T(8,128)(2,1)}, u32[]{:S(2)}) copy-start(bf16[2,128,128]{2,1,0:T(8,128)(2,1)} %param.12) | copy-start | bytes 196612
  9.2 435.6 %all-to-all-start = ((bf16[64,2,32,128]{3,2,1,0:T(8,128)(2,1)}), bf16[64,2,32,128]{3,2,1,0:T(8,128)(2,1)S(1)}, u32[]{:S(2)}, u32[]{:S(2)}) async-start(bf16[64,2,32,128]{3,2,1,0:T(8,128)(2,1)} %stack.2), calls=%async_computation | async-start | bytes 2097152 | tf_op jit(solution)/shard_map/all_to_all | solution.py:52
  25.9 381.3 %all-reduce.2.cloned.1.call-start = ((), (), s32[]{:S(2)}) async-start(), calls=%async_computation.2 | async-start | bytes 1048576 | tf_op jit(solution)/shard_map/psum | solution.py:77
  252.9 190.7 %reduce-scatter.2.cloned.1.call-start = ((), (), s32[]{:S(2)}) async-start(), calls=%async_computation.3 | async-start | bytes 73728 | tf_op jit(solution)/shard_map/reduce_scatter | solution.py:82
  445.1 1.1 copy-start.5
  445.1 1.1 copy-start.6
  445.1 1.1 copy-start.7
Sparse Core Ops, SparseCore 0:
  253.0 154.1 all-reduce.1
  410.6 32.8 reduce-scatter.1
